TPU v7x, 128 devices: a whole 4x4x4 slice. The times are simulated.
128 devices in a mesh: row: 32 (over x, y, core), col: 4 (over z).
Axes of the slice: x: 4, y: 4, z: 4, core: 2. Of those that a mesh axis runs over, the one named last changes fastest.
Arguments:
- right_side: bfloat16 [65536, 4096], P(('row', 'col')), may hold values from -6 to 6
- factor: bfloat16 [65536, 2048], P(('row', 'col')), may hold values from -0.125 to 0.125
- diag_inverse: bfloat16 [2048, 512], P('col'), as said below
- tile_mask: int32 [128, 4], P(('row', 'col')), may hold values from 0 to 1, as said below
- window_rows: int32 [4], replicated, may hold values from 0 to 127, as said below
Outputs:
- solution: bfloat16 [2048, 4096], P('row', 'col')
- updated_rhs: bfloat16 [65536, 4096], P(('row', 'col'))
Inputs may be any that keep to these rules, and one draw needn't show every extreme that they name: `window_rows`: distinct stored panel numbers, panels 0 and 127 always among them; panel p is stored on device p // 1 of row+col, and the window panels lie on different devices. `tile_mask`: 0 or 1; in the row of window panel k the entries of columns k and beyond are 0. `diag_inverse`: each tile is lower triangular.
All inputs are finite; a program needn't handle non-finite values.
Results may differ from a plain program's by a relative error of at most 0.0056.
Values may be sent and summed in bfloat16 or wider, within the bound.
A program may use at most 128 MiB of HBM per device.

v0:
```python
import jax
import jax.numpy as jnp
from jax import lax
from jax.sharding import PartitionSpec as P


def spread(block, axis, source):
    block = jnp.where(lax.axis_index(axis) == source, block, jnp.zeros_like(block))
    return lax.psum(block, axis)


def tile_term(flag, tile, panel_solution):
    zeros = jnp.zeros((tile.shape[0], panel_solution.shape[1]), jnp.float32)
    return lax.cond(
        flag > 0,
        lambda: jnp.dot(tile, panel_solution, preferred_element_type=jnp.float32),
        lambda: zeros,
    )


def body(right_side, factor, diag_inverse, tile_mask, window_rows):
    panel = diag_inverse.shape[1]
    window = factor.shape[1] // panel
    pan_dev = factor.shape[0] // panel
    columns = right_side.shape[1]
    ncol = lax.axis_size("col")
    nrow = lax.axis_size("row")
    inverses = lax.all_gather(diag_inverse, "col", axis=0, tiled=True).reshape(window, panel, panel)
    col_index = lax.axis_index("col")
    row_index = lax.axis_index("row")
    accum = jnp.zeros((pan_dev * panel, columns), jnp.float32)
    solved = []
    for k in range(window):
        target = window_rows[k]
        owner = target // pan_dev
        update = accum
        residual = right_side.astype(jnp.float32) - update
        rounded = residual.astype(jnp.bfloat16)
        local_solution = jnp.dot(inverses[k], rounded, preferred_element_type=jnp.float32).astype(
            jnp.bfloat16
        )
        solution_panel = spread(local_solution, ("row", "col"), owner)
        solved.append(solution_panel)
        tile = factor[0:panel, k * panel : (k + 1) * panel]
        term = tile_term(tile_mask[0, k], tile, solution_panel)
        accum = accum.at[0:panel].add(term)
    whole = jnp.concatenate(solved, axis=0)
    updated = (right_side.astype(jnp.float32) - accum).astype(jnp.bfloat16)
    block_rows = whole.shape[0] // nrow
    block_cols = columns // ncol
    solution = lax.dynamic_slice(
        whole, (row_index * block_rows, col_index * block_cols), (block_rows, block_cols)
    )
    return (solution, updated)


def solution(mesh):
    in_specs = (
        P(("row", "col"), None),
        P(("row", "col"), None),
        P("col", None),
        P(("row", "col"), None),
        P(),
    )
    out_specs = (P("row", "col"), P(("row", "col"), None))
    return jax.shard_map(body, mesh=mesh, in_specs=in_specs, out_specs=out_specs, check_vma=False)
```

profile of v0, /device:TPU:1, one launch (start us, length us, event | category | flops | bytes accessed | tf_op | source)
XLA Modules:
  0.0 760.8 jit_solution(18041693883802960980)
XLA Ops:
  7.2 0.0 all-gather.2.cloned.1.call-start
  7.2 0.7 all-gather.2.cloned.1.call-update
  7.9 0.0 all-reduce.5.cloned.1.call-start
  8.0 1.5 fusion.30
  10.1 33.9 %all-gather.2.cloned.1.call-done = bf16[2048,512]{1,0:T(8,128)(2,1)} async-done(((bf16[512,512]{1,0:T(8,128)(2,1)}), bf16[2048,512]{1,0:T(8,128)(2,1)}) %all-gather.2.cloned.1.call-update) | async-done | bytes 2097168 | tf_op jit(solution)/shard_map/all_gather | solution.py:28
  44.0 6.7 fusion.12
  50.7 0.0 copy-start.3
  50.7 0.0 copy-start.2
  50.7 0.0 all-reduce.5.cloned.1.call-update
  50.7 0.0 all-reduce.7.cloned.1.call-start
  50.8 0.6 copy-done.3
  51.3 0.7 fusion.29
  53.3 151.5 %all-reduce.5.cloned.1.call-done = bf16[512,4096]{1,0:T(8,128)(2,1)} async-done(((bf16[512,4096]{1,0:T(8,128)(2,1)}), bf16[512,4096]{1,0:T(8,128)(2,1)}) %all-reduce.5.cloned.1.call-update) | async-done | bytes 4194320 | tf_op jit(solution)/shard_map/psum | solution.py:9
  204.8 0.0 copy-done.2
  204.8 7.8 %conditional.4 = (f32[512,4096]{1,0:T(8,128)}) conditional(s32[]{:T(128)} %bitcast.2, () %tuple.68, (bf16[512,2048]{1,0:T(8,128)(2,1)S(1)}, bf16[512,4096]{1,0:T(8,128)(2,1)}) %tuple.101), branch_computations={%region_1.2_spmd, %region_2.3_spmd} | conditional | flops 2147483648 | bytes 13107208 | solution.py:14
  204.8 7.8 %fusion = f32[512,4096]{1,0:T(8,128)} fusion(bf16[512,4096]{1,0:T(8,128)(2,1)} %get-tuple-element.117, bf16[512,2048]{1,0:T(8,128)(2,1)S(1)} %get-tuple-element.116), kind=kOutput, calls=%fused_computation | convolution fusion | flops 2147483648 | bytes 13107200 | tf_op jit(solution)/shard_map/cond/branch_1_fun/dot_general | solution.py:16
  212.6 9.1 %fusion.14 = bf16[512,4096]{1,0:T(8,128)(2,1)} fusion(f32[512,4096]{1,0:T(8,128)} %get-tuple-element.134, bf16[512,4096]{1,0:T(8,128)(2,1)} %param.29, pred[]{:T(512)S(6)} %eq.13, bf16[2048,512]{1,0:T(8,128)(2,1)} %all-gather.2.cloned.1.call-done), kind=kOutput, calls=%fused_computation.26 | convolution fusion | flops 2157969408 | bytes 17301504 | tf_op jit(solution)/shard_map/dot_general | solution.py:39
  221.7 0.0 all-reduce.7.cloned.1.call-update
  221.7 0.0 all-reduce.9.cloned.1.call-start
  223.0 151.3 %all-reduce.7.cloned.1.call-done = bf16[512,4096]{1,0:T(8,128)(2,1)} async-done(((bf16[512,4096]{1,0:T(8,128)(2,1)}), bf16[512,4096]{1,0:T(8,128)(2,1)}) %all-reduce.7.cloned.1.call-update) | async-done | bytes 4194320 | tf_op jit(solution)/shard_map/psum | solution.py:9
  374.3 4.3 conditional.5
  374.3 4.3 broadcast.115
  378.6 0.0 copy-start
  378.6 11.3 %add.59 = f32[512,4096]{1,0:T(8,128)} add(f32[512,4096]{1,0:T(8,128)} %get-tuple-element.134, f32[512,4096]{1,0:T(8,128)} %get-tuple-element.135) | non-fusion elementwise | flops 2097152 | bytes 25165824 | tf_op jit(solution)/shard_map/add | solution.py:46
  389.9 0.0 copy-done
  389.9 8.1 %fusion.16 = bf16[512,4096]{1,0:T(8,128)(2,1)} fusion(f32[512,4096]{1,0:T(8,128)} %add.59, bf16[512,4096]{1,0:T(8,128)(2,1)S(1)} %copy-done, pred[]{:T(512)S(6)} %eq.14, bf16[2048,512]{1,0:T(8,128)(2,1)} %all-gather.2.cloned.1.call-done), kind=kOutput, calls=%fused_computation.28 | convolution fusion | flops 2157969408 | bytes 17301504 | tf_op jit(solution)/shard_map/dot_general | solution.py:39
  398.0 0.0 all-reduce.9.cloned.1.call-update
  398.0 0.0 all-reduce.11.cloned.1.call-start
  399.3 154.3 %all-reduce.9.cloned.1.call-done = bf16[512,4096]{1,0:T(8,128)(2,1)} async-done(((bf16[512,4096]{1,0:T(8,128)(2,1)}), bf16[512,4096]{1,0:T(8,128)(2,1)}) %all-reduce.9.cloned.1.call-update) | async-done | bytes 4194320 | tf_op jit(solution)/shard_map/psum | solution.py:9
  553.7 7.8 %conditional.6 = (f32[512,4096]{1,0:T(8,128)}) conditional(s32[]{:T(128)} %bitcast.8, () %tuple.72, (bf16[512,2048]{1,0:T(8,128)(2,1)S(1)}, bf16[512,4096]{1,0:T(8,128)(2,1)}) %tuple.103), branch_computations={%region_7.8_spmd, %region_8.9_spmd} | conditional | flops 2147483648 | bytes 13107208 | solution.py:14
  553.7 7.8 %fusion.4 = f32[512,4096]{1,0:T(8,128)} fusion(bf16[512,4096]{1,0:T(8,128)(2,1)} %get-tuple-element.121, bf16[512,2048]{1,0:T(8,128)(2,1)S(1)} %get-tuple-element.120), kind=kOutput, calls=%fused_computation.4 | convolution fusion | flops 2147483648 | bytes 13107200 | tf_op jit(solution)/shard_map/cond/branch_1_fun/dot_general | solution.py:16
  561.4 0.0 copy-start.1
  561.4 11.3 %add.60 = f32[512,4096]{1,0:T(8,128)} add(f32[512,4096]{1,0:T(8,128)} %add.59, f32[512,4096]{1,0:T(8,128)} %get-tuple-element.136) | non-fusion elementwise | flops 2097152 | bytes 25165824 | tf_op jit(solution)/shard_map/add | solution.py:46
  572.7 0.0 copy-done.1
  572.7 8.1 %fusion.18 = bf16[512,4096]{1,0:T(8,128)(2,1)} fusion(f32[512,4096]{1,0:T(8,128)} %add.60, bf16[512,4096]{1,0:T(8,128)(2,1)S(1)} %copy-done.1, pred[]{:T(512)S(6)} %eq.15, bf16[2048,512]{1,0:T(8,128)(2,1)} %all-gather.2.cloned.1.call-done), kind=kOutput, calls=%fused_computation.30 | convolution fusion | flops 2157969408 | bytes 17301504 | tf_op jit(solution)/shard_map/dot_general | solution.py:39
  580.9 0.0 all-reduce.11.cloned.1.call-update
  581.5 151.9 %all-reduce.11.cloned.1.call-done = bf16[512,4096]{1,0:T(8,128)(2,1)} async-done(((bf16[512,4096]{1,0:T(8,128)(2,1)}), bf16[512,4096]{1,0:T(8,128)(2,1)}) %all-reduce.11.cloned.1.call-update) | async-done | bytes 4194320 | tf_op jit(solution)/shard_map/psum | solution.py:9
  733.5 7.8 %conditional.7 = (f32[512,4096]{1,0:T(8,128)}) conditional(s32[]{:T(128)} %bitcast.10, () %tuple.74, (bf16[512,2048]{1,0:T(8,128)(2,1)S(1)}, bf16[512,4096]{1,0:T(8,128)(2,1)}) %tuple.104), branch_computations={%region_10.11_spmd, %region_11.12_spmd} | conditional | flops 2147483648 | bytes 13107208 | solution.py:14
  733.5 7.8 %fusion.6 = f32[512,4096]{1,0:T(8,128)} fusion(bf16[512,4096]{1,0:T(8,128)(2,1)} %get-tuple-element.123, bf16[512,2048]{1,0:T(8,128)(2,1)S(1)} %get-tuple-element.122), kind=kOutput, calls=%fused_computation.6 | convolution fusion | flops 2147483648 | bytes 13107200 | tf_op jit(solution)/shard_map/cond/branch_1_fun/dot_general | solution.py:16
  741.3 11.3 %fusion.11 = bf16[512,4096]{1,0:T(8,128)(2,1)} fusion(bf16[512,4096]{1,0:T(8,128)(2,1)} %param.29, f32[512,4096]{1,0:T(8,128)} %add.60, f32[512,4096]{1,0:T(8,128)} %get-tuple-element.137), kind=kLoop, calls=%fused_computation.19 | loop fusion | flops 8388608 | bytes 25165824 | tf_op jit(solution)/shard_map/convert_element_type | solution.py:48
  752.6 1.7 fusion.28
Async XLA Ops:
  7.2 36.8 %all-gather.2.cloned.1.call-start = ((), (), s32[]{:S(2)}) async-start(), calls=%async_computation | async-start | bytes 2621440 | tf_op jit(solution)/shard_map/all_gather | solution.py:28
  7.9 196.9 %all-reduce.5.cloned.1.call-start = ((), (), s32[]{:S(2)}) async-start(), calls=%async_computation.1 | async-start | bytes 8388608 | tf_op jit(solution)/shard_map/psum | solution.py:9
  50.7 0.7 copy-start.3
  50.7 154.1 %copy-start.2 = (bf16[512,2048]{1,0:T(8,128)(2,1)S(1)}, bf16[512,2048]{1,0:T(8,128)(2,1)}, u32[]{:S(2)}) copy-start(bf16[512,2048]{1,0:T(8,128)(2,1)} %param.30) | copy-start | bytes 6291460
  50.7 323.6 %all-reduce.7.cloned.1.call-start = ((), (), s32[]{:S(2)}) async-start(), calls=%async_computation.2 | async-start | bytes 8388608 | tf_op jit(solution)/shard_map/psum | solution.py:9
  221.7 331.9 %all-reduce.9.cloned.1.call-start = ((), (), s32[]{:S(2)}) async-start(), calls=%async_computation.3 | async-start | bytes 8388608 | tf_op jit(solution)/shard_map/psum | solution.py:9
  378.6 11.3 %copy-start = (bf16[512,4096]{1,0:T(8,128)(2,1)S(1)}, bf16[512,4096]{1,0:T(8,128)(2,1)}, u32[]{:S(2)}) copy-start(bf16[512,4096]{1,0:T(8,128)(2,1)} %param.29) | copy-start | bytes 12582916
  398.0 335.4 %all-reduce.11.cloned.1.call-start = ((), (), s32[]{:S(2)}) async-start(), calls=%async_computation.4 | async-start | bytes 8388608 | tf_op jit(solution)/shard_map/psum | solution.py:9
  561.4 11.3 %copy-start.1 = (bf16[512,4096]{1,0:T(8,128)(2,1)S(1)}, bf16[512,4096]{1,0:T(8,128)(2,1)}, u32[]{:S(2)}) copy-start(bf16[512,4096]{1,0:T(8,128)(2,1)} %param.29) | copy-start | bytes 12582916
Sparse Core Ops, SparseCore 0:
  9.7 34.2 all-gather.1
  50.8 153.9 all-reduce.4
  221.9 152.4 all-reduce.6
  398.1 155.4 all-reduce.8
  581.0 152.4 all-reduce.10
where the time goes:
time: 761 us
  waiting for transfers between devices  644 us (85%)
  matrix products  55.5 us (7%)
  other arithmetic  35.6 us (5%)
  between operations  18.9 us (2%)
    psum x4, waiting for transfers between devices, spread(): return lax.psum(block, axis)  609 us
    all_gather x1, waiting for transfers between devices, body(): lax.all_gather(diag_inverse, 'col', axis=0, tiled=True)  33.9 us
    dot_general x4, matrix products, body(): jnp.dot(inverses[k], rounded, preferred_element_type=jnp.float32)  32.1 us
    dot_general x3, matrix products, tile_term(): jnp.dot(tile, panel_solution, preferred_element_type=jnp.float32)  23.4 us
    add x2, other arithmetic, body(): accum = accum.at[0:panel].add(term)  22.6 us
  transfers between devices with their start and end apart: 5, of which 5 were waited for; matrix products, arithmetic and copies ran while one was open for 0% of the time, Pallas kernels for 0%

commit v1 on v0

--- a/solution.py
+++ b/solution.py
@@ -25,7 +25,46 @@
     columns = right_side.shape[1]
     ncol = lax.axis_size("col")
     nrow = lax.axis_size("row")
-    inverses = lax.all_gather(diag_inverse, "col", axis=0, tiled=True).reshape(window, panel, panel)
+
+    def series_all_bind(matrix, where_dim=0):
+        mesh_name = "col"
+        next_value, near, z_new = (
+            lax.axis_size(mesh_name),
+            lax.axis_index(mesh_name),
+            matrix.shape[where_dim],
+        )
+        log = []
+        for i0, dd in enumerate(matrix.shape):
+            log.append(dd * next_value if i0 == where_dim else dd)
+        piece_now = lax.dynamic_update_slice_in_dim(
+            jnp.zeros(log, matrix.dtype), matrix, near * z_new, axis=where_dim
+        )
+        low = local_out = matrix
+        u = 1
+        while u < next_value // 2 + 1:
+            trail = []
+            i0 = 0
+            while i0 < next_value:
+                trail.append((i0, (i0 + 1) % next_value))
+                i0 = i0 + 1
+            low = lax.ppermute(low, axis_name=mesh_name, perm=trail)
+            piece_now = lax.dynamic_update_slice_in_dim(
+                piece_now, low, (near - u) % next_value * z_new, axis=where_dim
+            )
+            if 2 * u < next_value:
+                stack_in = []
+                i0 = 0
+                while i0 < next_value:
+                    stack_in.append((i0, (i0 - 1) % next_value))
+                    i0 += 1
+                local_out = lax.ppermute(local_out, axis_name=mesh_name, perm=stack_in)
+                piece_now = lax.dynamic_update_slice_in_dim(
+                    piece_now, local_out, (near + u) % next_value * z_new, axis=where_dim
+                )
+            u = u + 1
+        return piece_now
+
+    inverses = series_all_bind(diag_inverse).reshape(window, panel, panel)
     col_index = lax.axis_index("col")
     row_index = lax.axis_index("row")
     accum = jnp.zeros((pan_dev * panel, columns), jnp.float32)

time: 761 us -> 754 us (level)
  waiting for transfers between devices: 644 us -> 630 us
    all_gather x1 -> x0, waiting for transfers between devices: 33.9 us -> none  [body(): lax.all_gather(diag_inverse, 'col', axis=0, tiled=True)]
    ppermute x0 -> x3, waiting for transfers between devices: none -> 20.6 us  [the longest x2 20.6 us: series_all_bind(): low = lax.ppermute(low, axis_name=mesh_name, perm=trail)]
  transfers between devices with their start and end apart: 5 -> 7, of which waited for: 5 -> 6; matrix products, arithmetic and copies ran while one was open for 0% -> 1% of each run, Pallas kernels for 0% -> 0%
where the time goes in v1:
time: 754 us
  waiting for transfers between devices  630 us (84%)
  matrix products  53 us (7%)
  other arithmetic  35.6 us (5%)
  between operations  19 us (3%)
  local copies, waits for them, and re-layouts  10.6 us (1%)
    psum x4, waiting for transfers between devices, spread(): return lax.psum(block, axis)  610 us
    dot_general x4, matrix products, body(): jnp.dot(inverses[k], rounded, preferred_element_type=jnp.float32)  29.2 us
    dot_general x3, matrix products, tile_term(): jnp.dot(tile, panel_solution, preferred_element_type=jnp.float32)  23.9 us
    add x2, other arithmetic, body(): accum = accum.at[0:panel].add(term)  22.6 us
    ppermute x2, waiting for transfers between devices, series_all_bind(): low = lax.ppermute(low, axis_name=mesh_name, perm=trail)  20.6 us
  transfers between devices with their start and end apart: 7, of which 6 were waited for; matrix products, arithmetic and copies ran while one was open for 1% of the time, Pallas kernels for 0%

profile of v1, /device:TPU:1, one launch (start us, length us, event | category | flops | bytes accessed | tf_op | source)
XLA Modules:
  0.0 753.5 jit_solution(12515864056173875590)
XLA Ops:
  7.2 0.0 all-reduce.5.cloned.1.call-start
  7.2 2.5 collective-permute-start
  9.7 2.2 collective-permute-start.1
  11.9 11.8 %collective-permute-done = bf16[512,512]{1,0:T(8,128)(2,1)S(1)} collective-permute-done((bf16[512,512]{1,0:T(8,128)(2,1)}, bf16[512,512]{1,0:T(8,128)(2,1)S(1)}, u32[]{:S(2)}, u32[]{:S(2)}) %collective-permute-start) | collective-permute-done | bytes 524320 | tf_op jit(solution)/shard_map/ppermute | solution.py:50
  23.7 0.0 collective-permute-start.2
  23.7 1.5 fusion.27
  25.8 0.0 copy-start
  25.9 0.1 broadcast_in_dim.3
  26.0 1.2 constant_dynamic-update-slice_fusion.3
  27.3 0.0 collective-permute-done.1
  27.3 1.1 constant_dynamic-update-slice_fusion.1
  28.4 8.8 %collective-permute-done.2 = bf16[512,512]{1,0:T(8,128)(2,1)} collective-permute-done((bf16[512,512]{1,0:T(8,128)(2,1)S(1)}, bf16[512,512]{1,0:T(8,128)(2,1)}, u32[]{:S(2)}, u32[]{:S(2)}) %collective-permute-start.2) | collective-permute-done | bytes 524320 | tf_op jit(solution)/shard_map/ppermute | solution.py:50
  37.2 1.1 constant_dynamic-update-slice_fusion
  38.3 0.0 copy-done
  38.3 4.4 fusion.12
  42.7 0.0 copy-start.3
  42.7 0.0 all-reduce.5.cloned.1.call-update
  42.7 0.0 all-reduce.7.cloned.1.call-start
  42.8 0.6 copy-done.3
  43.3 0.7 fusion.26
  45.3 152.0 %all-reduce.5.cloned.1.call-done = bf16[512,4096]{1,0:T(8,128)(2,1)} async-done(((bf16[512,4096]{1,0:T(8,128)(2,1)}), bf16[512,4096]{1,0:T(8,128)(2,1)}) %all-reduce.5.cloned.1.call-update) | async-done | bytes 4194320 | tf_op jit(solution)/shard_map/psum | solution.py:9
  197.4 8.0 %conditional.4 = (f32[512,4096]{1,0:T(8,128)}) conditional(s32[]{:T(128)} %bitcast.2, () %tuple.68, (bf16[512,2048]{1,0:T(8,128)(2,1)}, bf16[512,4096]{1,0:T(8,128)(2,1)}) %tuple.69), branch_computations={%region_1.2_spmd, %region_2.3_spmd} | conditional | flops 2147483648 | bytes 13107208 | solution.py:14
  197.4 8.0 %fusion = f32[512,4096]{1,0:T(8,128)} fusion(bf16[512,4096]{1,0:T(8,128)(2,1)} %get-tuple-element.117, bf16[512,2048]{1,0:T(8,128)(2,1)} %get-tuple-element.116), kind=kOutput, calls=%fused_computation | convolution fusion | flops 2147483648 | bytes 13107200 | tf_op jit(solution)/shard_map/cond/branch_1_fun/dot_general | solution.py:16
  205.3 9.0 %fusion.13 = bf16[512,4096]{1,0:T(8,128)(2,1)} fusion(f32[512,4096]{1,0:T(8,128)} %get-tuple-element.134, bf16[512,4096]{1,0:T(8,128)(2,1)} %param.29, pred[]{:T(512)S(6)} %eq.17, bf16[2048,512]{1,0:T(8,128)(2,1)S(1)} %constant_dynamic-update-slice_fusion), kind=kOutput, calls=%fused_computation.25 | convolution fusion | flops 2157969408 | bytes 17301504 | tf_op jit(solution)/shard_map/dot_general | solution.py:78
  214.3 0.0 all-reduce.7.cloned.1.call-update
  214.3 0.0 all-reduce.9.cloned.1.call-start
  215.6 151.3 %all-reduce.7.cloned.1.call-done = bf16[512,4096]{1,0:T(8,128)(2,1)} async-done(((bf16[512,4096]{1,0:T(8,128)(2,1)}), bf16[512,4096]{1,0:T(8,128)(2,1)}) %all-reduce.7.cloned.1.call-update) | async-done | bytes 4194320 | tf_op jit(solution)/shard_map/psum | solution.py:9
  366.9 4.3 conditional.5
  366.9 4.3 broadcast.107
  371.1 0.0 copy-start.1
  371.1 11.3 %add.94 = f32[512,4096]{1,0:T(8,128)} add(f32[512,4096]{1,0:T(8,128)} %get-tuple-element.134, f32[512,4096]{1,0:T(8,128)} %get-tuple-element.135) | non-fusion elementwise | flops 2097152 | bytes 25165824 | tf_op jit(solution)/shard_map/add | solution.py:85
  382.4 0.0 copy-done.1
  382.4 7.9 %fusion.14 = bf16[512,4096]{1,0:T(8,128)(2,1)} fusion(f32[512,4096]{1,0:T(8,128)} %add.94, bf16[512,4096]{1,0:T(8,128)(2,1)S(1)} %copy-done.1, pred[]{:T(512)S(6)} %eq.18, bf16[2048,512]{1,0:T(8,128)(2,1)S(1)} %constant_dynamic-update-slice_fusion), kind=kOutput, calls=%fused_computation.26 | convolution fusion | flops 2157969408 | bytes 17301504 | tf_op jit(solution)/shard_map/dot_general | solution.py:78
  390.4 0.0 all-reduce.9.cloned.1.call-update
  390.4 0.0 all-reduce.11.cloned.1.call-start
  391.7 154.5 %all-reduce.9.cloned.1.call-done = bf16[512,4096]{1,0:T(8,128)(2,1)} async-done(((bf16[512,4096]{1,0:T(8,128)(2,1)}), bf16[512,4096]{1,0:T(8,128)(2,1)}) %all-reduce.9.cloned.1.call-update) | async-done | bytes 4194320 | tf_op jit(solution)/shard_map/psum | solution.py:9
  546.2 8.0 %conditional.6 = (f32[512,4096]{1,0:T(8,128)}) conditional(s32[]{:T(128)} %bitcast.6, () %tuple.72, (bf16[512,2048]{1,0:T(8,128)(2,1)}, bf16[512,4096]{1,0:T(8,128)(2,1)}) %tuple.73), branch_computations={%region_7.8_spmd, %region_8.9_spmd} | conditional | flops 2147483648 | bytes 13107208 | solution.py:14
  546.2 8.0 %fusion.4 = f32[512,4096]{1,0:T(8,128)} fusion(bf16[512,4096]{1,0:T(8,128)(2,1)} %get-tuple-element.121, bf16[512,2048]{1,0:T(8,128)(2,1)} %get-tuple-element.120), kind=kOutput, calls=%fused_computation.4 | convolution fusion | flops 2147483648 | bytes 13107200 | tf_op jit(solution)/shard_map/cond/branch_1_fun/dot_general | solution.py:16
  554.2 0.0 copy-start.2
  554.2 11.3 %add.95 = f32[512,4096]{1,0:T(8,128)} add(f32[512,4096]{1,0:T(8,128)} %add.94, f32[512,4096]{1,0:T(8,128)} %get-tuple-element.136) | non-fusion elementwise | flops 2097152 | bytes 25165824 | tf_op jit(solution)/shard_map/add | solution.py:85
  565.5 0.0 copy-done.2
  565.5 7.9 %fusion.15 = bf16[512,4096]{1,0:T(8,128)(2,1)} fusion(f32[512,4096]{1,0:T(8,128)} %add.95, bf16[512,4096]{1,0:T(8,128)(2,1)S(1)} %copy-done.2, pred[]{:T(512)S(6)} %eq.19, bf16[2048,512]{1,0:T(8,128)(2,1)S(1)} %constant_dynamic-update-slice_fusion), kind=kOutput, calls=%fused_computation.27 | convolution fusion | flops 2157969408 | bytes 17301504 | tf_op jit(solution)/shard_map/dot_general | solution.py:78
  573.4 0.0 all-reduce.11.cloned.1.call-update
  574.1 151.9 %all-reduce.11.cloned.1.call-done = bf16[512,4096]{1,0:T(8,128)(2,1)} async-done(((bf16[512,4096]{1,0:T(8,128)(2,1)}), bf16[512,4096]{1,0:T(8,128)(2,1)}) %all-reduce.11.cloned.1.call-update) | async-done | bytes 4194320 | tf_op jit(solution)/shard_map/psum | solution.py:9
  726.0 8.0 %conditional.7 = (f32[512,4096]{1,0:T(8,128)}) conditional(s32[]{:T(128)} %bitcast.7, () %tuple.74, (bf16[512,2048]{1,0:T(8,128)(2,1)}, bf16[512,4096]{1,0:T(8,128)(2,1)}) %tuple.75), branch_computations={%region_10.11_spmd, %region_11.12_spmd} | conditional | flops 2147483648 | bytes 13107208 | solution.py:14
  726.0 8.0 %fusion.6 = f32[512,4096]{1,0:T(8,128)} fusion(bf16[512,4096]{1,0:T(8,128)(2,1)} %get-tuple-element.123, bf16[512,2048]{1,0:T(8,128)(2,1)} %get-tuple-element.122), kind=kOutput, calls=%fused_computation.6 | convolution fusion | flops 2147483648 | bytes 13107200 | tf_op jit(solution)/shard_map/cond/branch_1_fun/dot_general | solution.py:16
  734.0 11.3 %fusion.11 = bf16[512,4096]{1,0:T(8,128)(2,1)} fusion(bf16[512,4096]{1,0:T(8,128)(2,1)} %param.29, f32[512,4096]{1,0:T(8,128)} %add.95, f32[512,4096]{1,0:T(8,128)} %get-tuple-element.137), kind=kLoop, calls=%fused_computation.19 | loop fusion | flops 8388608 | bytes 25165824 | tf_op jit(solution)/shard_map/convert_element_type | solution.py:87
  745.3 1.7 fusion.25
  (1 shorter events, 0.0 us)
Async XLA Ops:
  7.2 190.2 %all-reduce.5.cloned.1.call-start = ((), (), s32[]{:S(2)}) async-start(), calls=%async_computation | async-start | bytes 8388608 | tf_op jit(solution)/shard_map/psum | solution.py:9
  7.2 16.5 %collective-permute-start = (bf16[512,512]{1,0:T(8,128)(2,1)}, bf16[512,512]{1,0:T(8,128)(2,1)S(1)}, u32[]{:S(2)}, u32[]{:S(2)}) collective-permute-start(bf16[512,512]{1,0:T(8,128)(2,1)} %param.31), channel_id=1, source_target_pairs={{0,1},{1,2},{2,3},{3,0},{4,5},{5,6},{6,7},{7,4},{8,9},{9,10},{10,1... | collective-permute-start | bytes 1572872 | tf_op jit(solution)/shard_map/ppermute | solution.py:50
  9.7 17.5 %collective-permute-start.1 = (bf16[512,512]{1,0:T(8,128)(2,1)}, bf16[512,512]{1,0:T(8,128)(2,1)}, u32[]{:S(2)}, u32[]{:S(2)}) collective-permute-start(bf16[512,512]{1,0:T(8,128)(2,1)} %param.31), channel_id=1, source_target_pairs={{0,3},{1,0},{2,1},{3,2},{4,7},{5,4},{6,5},{7,6},{8,11},{9,8},{10,9... | collective-permute-start | bytes 1572872 | tf_op jit(solution)/shard_map/ppermute | solution.py:60
  23.7 13.5 %collective-permute-start.2 = (bf16[512,512]{1,0:T(8,128)(2,1)S(1)}, bf16[512,512]{1,0:T(8,128)(2,1)}, u32[]{:S(2)}, u32[]{:S(2)}) collective-permute-start(bf16[512,512]{1,0:T(8,128)(2,1)S(1)} %collective-permute-done), channel_id=1, source_target_pairs={{0,1},{1,2},{2,3},{3,0},{4,5},{5,6},{6,7},{7,4},{8,9},{9,10},{10,1... | collective-permute-start | bytes 1572872 | tf_op jit(solution)/shard_map/ppermute | solution.py:50
  25.8 12.5 %copy-start = (bf16[512,4096]{1,0:T(8,128)(2,1)S(1)}, bf16[512,4096]{1,0:T(8,128)(2,1)}, u32[]{:S(2)}) copy-start(bf16[512,4096]{1,0:T(8,128)(2,1)} %param.29) | copy-start | bytes 12582916
  42.7 0.7 copy-start.3
  42.7 324.2 %all-reduce.7.cloned.1.call-start = ((), (), s32[]{:S(2)}) async-start(), calls=%async_computation.1 | async-start | bytes 8388608 | tf_op jit(solution)/shard_map/psum | solution.py:9
  214.3 331.9 %all-reduce.9.cloned.1.call-start = ((), (), s32[]{:S(2)}) async-start(), calls=%async_computation.2 | async-start | bytes 8388608 | tf_op jit(solution)/shard_map/psum | solution.py:9
  371.1 11.3 %copy-start.1 = (bf16[512,4096]{1,0:T(8,128)(2,1)S(1)}, bf16[512,4096]{1,0:T(8,128)(2,1)}, u32[]{:S(2)}) copy-start(bf16[512,4096]{1,0:T(8,128)(2,1)} %param.29) | copy-start | bytes 12582916
  390.4 335.6 %all-reduce.11.cloned.1.call-start = ((), (), s32[]{:S(2)}) async-start(), calls=%async_computation.3 | async-start | bytes 8388608 | tf_op jit(solution)/shard_map/psum | solution.py:9
  554.2 11.3 %copy-start.2 = (bf16[512,4096]{1,0:T(8,128)(2,1)S(1)}, bf16[512,4096]{1,0:T(8,128)(2,1)}, u32[]{:S(2)}) copy-start(bf16[512,4096]{1,0:T(8,128)(2,1)} %param.29) | copy-start | bytes 12582916
Sparse Core Ops, SparseCore 0:
  42.8 154.4 all-reduce.4
  214.4 152.4 all-reduce.6
  390.5 155.6 all-reduce.8
  573.5 152.4 all-reduce.10
